TPU v7x, 32 devices: a whole 2x2x4 slice. The times are simulated.
32 devices in a mesh: groups: 2 (over x), ctx: 16 (over z, y, core).
Axes of the slice: x: 2, y: 2, z: 4, core: 2. Of those that a mesh axis runs over, the one named last changes fastest.
Arguments:
- queries: bfloat16 [8192, 1024], P(('groups', 'ctx')), parts along dimension 0, may hold values from -128 to 128
- keys: bfloat16 [8192, 128], P(('groups', 'ctx')), parts along dimension 0, may hold values from -32 to 32
- values: bfloat16 [8192, 128], P(('groups', 'ctx')), parts along dimension 0, may hold values from -6 to 6
- doc_ids: int32 [8192], P(('groups', 'ctx')), parts along dimension 0, may hold values from 0 to 2, never falling along the last dimension, each value on 1 to 3072 neighbouring positions
Outputs:
- attended: bfloat16 [8192, 1024], P(('groups', 'ctx')), parts along dimension 0
There are 2 independent parts, one for each index of `groups`. A program takes and returns all parts, laid end to end along the dimension named above; each array names one. Nothing has to cross between parts.
All inputs are finite; a program needn't handle non-finite values.
Results may differ from a plain program's by a relative error of at most 0.0041.
Values may be sent and summed in bfloat16 or wider, within the bound.
A program may use at most 64 MiB of HBM per device.

v0:
```python
import functools

import jax
import jax.numpy as jnp
from jax import lax
from jax.experimental import pallas as pl
from jax.experimental.pallas import tpu as pltpu
from jax.sharding import PartitionSpec as P

HIDDEN = -1e30
LOG2E = 1.4426950408889634
TILE_HEADS = 2


def kernel(
    n,
    q_hbm,
    k_hbm,
    v_hbm,
    d_hbm,
    o_hbm,
    q_ref,
    o_ref,
    kv,
    docs,
    bias,
    m_ref,
    acc_ref,
    qs,
    fill_sem,
    out_sem,
    send_kv,
    recv_kv,
    send_doc,
    recv_doc,
):
    rows, width = q_hbm.shape
    dim = k_hbm.shape[1]
    heads = width // dim
    levels = n // 4
    window = 3 * n // 4
    depth = (window + 3) // 4
    me = lax.axis_index("ctx")
    z = me // 4
    r = me % 4
    y = r // 2
    c = r % 2
    chip = me // 2
    up = me + 4
    across = z * 4 + (1 - y) * 2 + c
    partner = z * 4 + y * 2 + (1 - c)
    scale = dim ** (-0.5) * LOG2E
    keys_wide = 2 * rows

    def span(block):
        return pl.ds(pl.multiple_of(block * rows, rows), rows)

    fills = [
        pltpu.make_async_copy(k_hbm, kv.at[0, span(me), :], fill_sem.at[0]),
        pltpu.make_async_copy(v_hbm, kv.at[1, span(me), :], fill_sem.at[1]),
        pltpu.make_async_copy(d_hbm, docs.at[me], fill_sem.at[2]),
    ]
    for fill in fills:
        fill.start()
    query_fill = pltpu.make_async_copy(q_hbm, q_ref, fill_sem.at[3])
    query_fill.start()

    barrier = pltpu.get_barrier_semaphore()

    def greet(device):
        pl.semaphore_signal(
            barrier, inc=1, device_id={"ctx": device}, device_id_type=pl.DeviceIdType.MESH
        )

    greet(partner)
    greet(across)

    @pl.when(z > 0)
    def _():
        greet(me - 4)

    @pl.when(z < levels - 1)
    def _():
        greet(up)

    pl.semaphore_wait(barrier, 2 + jnp.minimum(z, 1) + jnp.minimum(levels - 1 - z, 1))

    def copies(stream, level, piece, block, device):
        made = [
            pltpu.make_async_remote_copy(
                src_ref=kv.at[piece, span(block), :],
                dst_ref=kv.at[piece, span(block), :],
                send_sem=send_kv.at[stream, level, piece],
                recv_sem=recv_kv.at[stream, level, piece],
                device_id={"ctx": device},
                device_id_type=pl.DeviceIdType.MESH,
            )
        ]
        if piece == 0:
            made.append(
                pltpu.make_async_remote_copy(
                    src_ref=docs.at[block],
                    dst_ref=docs.at[block],
                    send_sem=send_doc.at[stream, level],
                    recv_sem=recv_doc.at[stream, level],
                    device_id={"ctx": device},
                    device_id_type=pl.DeviceIdType.MESH,
                )
            )
        return made

    def start(*where):
        for copy in copies(*where):
            copy.start()

    def arrived(*where):
        for copy in copies(*where):
            copy.wait_recv()

    def sent(*where):
        for copy in copies(*where):
            copy.wait_send()

    def needs(some_chip, chunk):
        return (chunk <= some_chip) & (2 * chunk + 1 >= 2 * some_chip - window)

    def climbs(level):
        return (z < levels - 1) & (z - level < depth)

    def crosses(level):
        return needs(2 * z + 1 - y, 2 * level + y)

    def crossed(level):
        return needs(chip, 2 * level + 1 - y)

    def relay(level, piece):
        block = level * 4 + r

        @pl.when(climbs(level))
        def _():
            start(0, level, piece, block, up)

        @pl.when(crosses(level))
        def _():
            start(1, level, piece, block, across)

        start(2, level, piece, block, partner)

    for fill in fills[:1] + fills[2:]:
        fill.wait()
    relay(z, 0)
    fills[1].wait()
    relay(z, 1)

    lane = lax.broadcasted_iota(jnp.int32, (rows, dim), 1)
    row_id = me * rows + lax.broadcasted_iota(jnp.int32, (rows, dim), 0)
    doc_col = jnp.broadcast_to(docs[me], (dim, rows)).T
    query_marks = jnp.where(lane == doc_col, 0.0, HIDDEN).astype(jnp.bfloat16)
    query_fill.wait()
    for head in range(heads):
        here = slice(head * rows, (head + 1) * rows)
        qs[here, :dim] = q_ref[:, head * dim : (head + 1) * dim]
        qs[here, dim:] = query_marks

    def attend(chunk, first, hooks):
        place = pl.ds(pl.multiple_of(chunk * keys_wide, keys_wide), keys_wide)
        marks = []
        for half in range(2):
            key_col = jnp.broadcast_to(docs[chunk * 2 + half], (dim, rows)).T
            marks.append(jnp.where(lane == key_col, 1.0, 0.0).astype(jnp.bfloat16))
        k_chunk = jnp.concatenate([kv[0, place, :], jnp.concatenate(marks, axis=0)], axis=1)
        v_chunk = jnp.concatenate(
            [kv[1, place, :], jnp.ones((keys_wide, dim), jnp.bfloat16)], axis=1
        )
        if first:
            for part in range(keys_wide // dim):
                key_id = chunk * keys_wide + part * dim + lane
                bias[:, part * dim : (part + 1) * dim] = jnp.where(key_id <= row_id, 0.0, HIDDEN)
        tile_rows = TILE_HEADS * rows

        def scores(tile):
            return lax.dot_general(
                qs[tile * tile_rows : (tile + 1) * tile_rows, :],
                k_chunk,
                (((1,), (1,)), ((), ())),
                preferred_element_type=jnp.float32,
            )

        tiles = heads // TILE_HEADS
        following = scores(0)
        for tile in range(tiles):
            s = following
            if tile + 1 < tiles:
                following = scores(tile + 1)
            here = slice(tile * tile_rows, (tile + 1) * tile_rows)
            if first:
                s = s + jnp.concatenate([bias[...]] * TILE_HEADS, axis=0)
            new = jnp.max(s, axis=1, keepdims=True)
            if first:
                new = jnp.broadcast_to(new, (tile_rows, dim))
            else:
                old = m_ref[here]
                new = jnp.maximum(old, new)
            m_ref[here] = new
            w = jnp.exp2((s - jnp.tile(new, (1, keys_wide // dim))) * scale)
            part = jnp.dot(w.astype(jnp.bfloat16), v_chunk, preferred_element_type=jnp.float32)
            if first:
                acc_ref[here] = part
            else:
                acc_ref[here] = (
                    acc_ref[here] * jnp.tile(jnp.exp2((old - new) * scale), (1, 2)) + part
                )
            if tile < len(hooks):
                hooks[tile]()

    def process(chunk, hooks=()):
        needed = (chunk <= chip) & (chunk * 2 + 1 >= me - window)

        @pl.when(needed)
        def _():
            attend(chunk, False, hooks)

        if hooks:

            @pl.when(jnp.logical_not(needed))
            def _():
                for hook in hooks:
                    hook()

    def from_below(level, piece):
        def hook():
            @pl.when(level > jnp.maximum(z - depth, 0))
            def _():
                arrived(0, level - 1, piece, (level - 1) * 4 + r, up)
                relay(level - 1, piece)

        return hook

    def from_across(level, piece):
        block = level * 4 + 2 * (1 - y) + c

        def hook():
            @pl.when(crossed(level))
            def _():
                arrived(1, level, piece, block, across)
                start(3, level, piece, block, partner)

        return hook

    def own_column(level):
        for piece in range(2):
            arrived(2, level, piece, level * 4 + 2 * y + 1 - c, partner)

    def other_column(level):
        @pl.when(crossed(level))
        def _():
            for piece in range(2):
                arrived(3, level, piece, level * 4 + 2 * (1 - y) + 1 - c, partner)

    def hooks_of(level):
        return (
            from_below(level, 0),
            from_below(level, 1),
            from_across(level, 0),
            from_across(level, 1),
        )

    own_column(z)
    attend(chip, True, hooks_of(z))

    def step(i, carry):
        level = z - i
        own_column(level)
        process(level * 2 + y, hooks_of(level))
        other_column(level + 1)
        process((level + 1) * 2 + 1 - y)
        return carry

    last = jnp.minimum(z, depth)
    lax.fori_loop(1, last + 1, step, 0)
    other_column(z - last)
    process((z - last) * 2 + 1 - y)

    def out_copy(head):
        cols = slice(head * dim, (head + 1) * dim)
        return pltpu.make_async_copy(o_ref.at[:, cols], o_hbm.at[:, cols], out_sem.at[head])

    for head in range(heads):
        here = slice(head * rows, (head + 1) * rows)
        o_ref[:, head * dim : (head + 1) * dim] = (acc_ref[here, :dim] / acc_ref[here, dim:]).astype(
            o_ref.dtype
        )
        out_copy(head).start()

    def finish(i, carry):
        level = z - i
        block = level * 4 + r
        for piece in range(2):

            @pl.when(climbs(level))
            def _():
                sent(0, level, piece, block, up)

            @pl.when(crosses(level))
            def _():
                sent(1, level, piece, block, across)

            sent(2, level, piece, block, partner)

            @pl.when(crossed(level))
            def _():
                sent(3, level, piece, level * 4 + 2 * (1 - y) + c, partner)

        return carry

    lax.fori_loop(0, last + 1, finish, 0)
    for head in range(heads):
        out_copy(head).wait()


def solution(mesh):
    n = mesh.shape["ctx"]

    def on_device(queries, keys, values, doc_ids):
        rows, width = queries.shape
        dim = keys.shape[1]
        heads = width // dim
        levels = n // 4
        anywhere = pl.BlockSpec(memory_space=pl.ANY)
        piece_sems = pltpu.SemaphoreType.DMA((4, levels, 2))
        doc_sems = pltpu.SemaphoreType.DMA((4, levels))
        return pl.pallas_call(
            functools.partial(kernel, n),
            out_shape=jax.ShapeDtypeStruct((rows, width), jnp.bfloat16),
            in_specs=[anywhere] * 4,
            out_specs=anywhere,
            scratch_shapes=[
                pltpu.VMEM((rows, width), jnp.bfloat16),
                pltpu.VMEM((rows, width), jnp.bfloat16),
                pltpu.VMEM((2, n * rows, dim), jnp.bfloat16),
                pltpu.VMEM((n, 1, rows), jnp.int32),
                pltpu.VMEM((rows, 2 * rows), jnp.float32),
                pltpu.VMEM((heads * rows, dim), jnp.float32),
                pltpu.VMEM((heads * rows, 2 * dim), jnp.float32),
                pltpu.VMEM((heads * rows, 2 * dim), jnp.bfloat16),
                pltpu.SemaphoreType.DMA((4,)),
                pltpu.SemaphoreType.DMA((heads,)),
                piece_sems,
                piece_sems,
                doc_sems,
                doc_sems,
            ],
            compiler_params=pltpu.CompilerParams(collective_id=0, has_side_effects=True, vmem_limit_bytes=16 * 1024 * 1024),
        )(*[pltpu.with_memory_space_constraint(a, pltpu.HBM) for a in (queries, keys, values, doc_ids.reshape(1, rows))])

    spec = P(("groups", "ctx"), None)
    return jax.shard_map(
        on_device,
        mesh=mesh,
        in_specs=(spec, spec, spec, P(("groups", "ctx"))),
        out_specs=spec,
        check_vma=False,
    )
```

profile of v0, /device:TPU:25, one launch (start us, length us, event | category | flops | bytes accessed | tf_op | source)
XLA Modules:
  0.0 22.1 jit_solution(15059823639331218540)
XLA Ops:
  0.0 21.3 %shard_map.46 = bf16[256,1024]{1,0:T(8,128)(2,1)S(1)} custom-call(bf16[256,1024]{1,0:T(8,128)(2,1)} %q_hbm.1, bf16[256,128]{1,0:T(8,128)(2,1)} %k_hbm.1, bf16[256,128]{1,0:T(8,128)(2,1)} %v_hbm.1, s32[1,256]{1,0:T(1,128)} %bitcast.1), custom_call_target="tpu_custom_call" | custom-call | tf_op jit(solution)/shard_map/pallas_call | solution.py:332
  21.3 0.8 %copy.6 = bf16[256,1024]{1,0:T(8,128)(2,1)} copy(bf16[256,1024]{1,0:T(8,128)(2,1)S(1)} %shard_map.46) | data formatting | bytes 1048576
where the time goes:
time: 22.5 us; the launch traced here: 22.1 us
  Pallas kernels  21.3 us (95%)
  local copies, waits for them, and re-layouts  0.8 us (4%)
    pallas_call x1, Pallas kernels, on_device(): pl.pallas_call(functools.partial(kernel, n), out_shape=jax.ShapeDtypeStru...  21.3 us
    unnamed x1, local copies, waits for them, and re-layouts  0.8 us

commit v1 on v0

v1 whole, which is shorter than its diff:
```python
import functools

import jax
import jax.numpy as jnp
from jax import lax
from jax.experimental import pallas as pl
from jax.experimental.pallas import tpu as pltpu
from jax.sharding import PartitionSpec as P

HIDDEN = -1e30
LOG2E = 1.4426950408889634
DOCS = 3
TILE_HEADS = 2


def kernel(
    n,
    q_hbm,
    k_hbm,
    v_hbm,
    d_hbm,
    o_ref,
    q_ref,
    kv,
    docs,
    m_ref,
    acc_ref,
    qs,
    fill_sem,
    send_kv,
    recv_kv,
    send_doc,
    recv_doc,
):
    rows, width = q_hbm.shape
    dim = k_hbm.shape[1]
    heads = width // dim
    levels = n // 4
    window = 3 * n // 4
    depth = (window + 3) // 4
    me = lax.axis_index("ctx")
    z = me // 4
    r = me % 4
    y = r // 2
    c = r % 2
    chip = me // 2
    up = me + 4
    across = z * 4 + (1 - y) * 2 + c
    partner = z * 4 + y * 2 + (1 - c)
    scale = dim ** (-0.5) * LOG2E
    top = z == levels - 1
    last = jnp.minimum(z, depth)

    barrier = pltpu.get_barrier_semaphore()

    def greet(device):
        pl.semaphore_signal(
            barrier, inc=1, device_id={"ctx": device}, device_id_type=pl.DeviceIdType.MESH
        )

    @pl.when(z > 0)
    def _():
        greet(me - 4)

    @pl.when(z < levels - 1)
    def _():
        greet(up)

    greet(across)
    greet(partner)

    def span(block):
        return pl.ds(pl.multiple_of(block * rows, rows), rows)

    fills = [
        pltpu.make_async_copy(k_hbm, kv.at[0, span(me), :], fill_sem.at[0]),
        pltpu.make_async_copy(v_hbm, kv.at[1, span(me), :], fill_sem.at[1]),
        pltpu.make_async_copy(d_hbm, docs.at[me], fill_sem.at[2]),
    ]
    for fill in fills:
        fill.start()
    query_fill = pltpu.make_async_copy(q_hbm, q_ref, fill_sem.at[3])
    query_fill.start()

    def copies(stream, lands, level, piece, block, device):
        made = [
            pltpu.make_async_remote_copy(
                src_ref=kv.at[piece, span(block), :],
                dst_ref=kv.at[piece, span(block), :],
                send_sem=send_kv.at[stream, level, piece],
                recv_sem=recv_kv.at[lands, level, piece],
                device_id={"ctx": device},
                device_id_type=pl.DeviceIdType.MESH,
            )
        ]
        if piece == 0:
            made.append(
                pltpu.make_async_remote_copy(
                    src_ref=docs.at[block],
                    dst_ref=docs.at[block],
                    send_sem=send_doc.at[stream, level],
                    recv_sem=recv_doc.at[lands, level],
                    device_id={"ctx": device},
                    device_id_type=pl.DeviceIdType.MESH,
                )
            )
        return made

    def start(stream, lands, *where):
        for copy in copies(stream, lands, *where):
            copy.start()

    def arrived(lands, *where):
        for copy in copies(lands, lands, *where):
            copy.wait_recv()

    def sent(stream, lands, *where):
        for copy in copies(stream, lands, *where):
            copy.wait_send()

    def needs(some_chip, chunk):
        return (chunk <= some_chip) & (2 * chunk + 1 >= 2 * some_chip - window)

    def from_under(some_z, some_y, level):
        return (some_y == 0) & (some_z - level == depth) & needs(2 * some_z, 2 * level + 1)

    def climbs(level):
        return (z < levels - 1) & (z - level < depth)

    def crosses(level):
        return needs(2 * z + 1 - y, 2 * level + y) & jnp.logical_not(from_under(z, 1 - y, level))

    def crossed(level):
        return needs(chip, 2 * level + 1 - y)

    def passes(level):
        return (z < levels - 1) & from_under(z + 1, y, level)

    def own(level):
        return level * 4 + r

    def other(level):
        return level * 4 + 2 * (1 - y) + c

    def relay(level, piece):
        @pl.when(climbs(level))
        def _():
            start(0, 0, level, piece, own(level), up)

        @pl.when(crosses(level))
        def _():
            start(1, 1, level, piece, own(level), across)

        start(2, 2, level, piece, own(level), partner)

    def from_below(level):
        for piece in range(2):
            arrived(0, level, piece, own(level), up)
            relay(level, piece)

    def from_across(level):
        @pl.when(crossed(level))
        def _():
            for piece in range(2):
                arrived(1, level, piece, other(level), across)

                @pl.when(passes(level))
                def _():
                    start(4, 1, level, piece, other(level), up)

                start(3, 3, level, piece, other(level), partner)

    def own_pair(level):
        for piece in range(2):
            arrived(2, level, piece, level * 4 + 2 * y + 1 - c, partner)

    def other_pair(level):
        @pl.when(crossed(level))
        def _():
            for piece in range(2):
                arrived(3, level, piece, level * 4 + 2 * (1 - y) + 1 - c, partner)

    def finish(level):
        for piece in range(2):

            @pl.when(climbs(level))
            def _():
                sent(0, 0, level, piece, own(level), up)

            @pl.when(crosses(level))
            def _():
                sent(1, 1, level, piece, own(level), across)

            sent(2, 2, level, piece, own(level), partner)

            @pl.when(crossed(level))
            def _():
                sent(3, 3, level, piece, other(level), partner)

                @pl.when(passes(level))
                def _():
                    sent(4, 1, level, piece, other(level), up)

    pl.semaphore_wait(barrier, 2 + jnp.minimum(z, 1) + jnp.minimum(levels - 1 - z, 1))
    for fill in fills[:1] + fills[2:]:
        fill.wait()
    relay(z, 0)
    fills[1].wait()
    relay(z, 1)

    lane = lax.broadcasted_iota(jnp.int32, (rows, dim), 1)
    row = lax.broadcasted_iota(jnp.int32, (rows, dim), 0)

    def doc_of(block):
        ids = docs[block]
        number = jnp.zeros((rows, dim), jnp.int32)
        for doc in range(1, DOCS):
            under = jnp.sum(jnp.where(ids < doc, 1.0, 0.0), axis=1, keepdims=True).astype(jnp.int32)
            number = number + jnp.where(row >= under, 1, 0)
        return number

    query_marks = jnp.where(lane == doc_of(me), 0.0, HIDDEN).astype(jnp.bfloat16)
    query_fill.wait()
    for head in range(heads):
        here = slice(head * rows, (head + 1) * rows)
        qs[here, :dim] = q_ref[:, head * dim : (head + 1) * dim]
        qs[here, dim:] = query_marks

    tile_rows = TILE_HEADS * rows
    tiles = heads // TILE_HEADS

    def attend(block, first=False):
        place = span(block)
        marks = jnp.where(lane == doc_of(block), 1.0, 0.0).astype(jnp.bfloat16)
        k_block = jnp.concatenate([kv[0, place, :], marks], axis=1)
        v_block = jnp.concatenate([kv[1, place, :], jnp.ones((rows, dim), jnp.bfloat16)], axis=1)

        def scores(tile):
            return lax.dot_general(
                qs[tile * tile_rows : (tile + 1) * tile_rows, :],
                k_block,
                (((1,), (1,)), ((), ())),
                preferred_element_type=jnp.float32,
            )

        following = scores(0)
        for tile in range(tiles):
            s = following
            if tile + 1 < tiles:
                following = scores(tile + 1)
            here = slice(tile * tile_rows, (tile + 1) * tile_rows)
            if first:
                key_id = lax.broadcasted_iota(jnp.int32, (rows, rows), 1)
                query_id = lax.broadcasted_iota(jnp.int32, (rows, rows), 0)
                hide = jnp.where(key_id <= query_id, 0.0, HIDDEN)
                s = s + jnp.concatenate([hide] * TILE_HEADS, axis=0)
            new = jnp.broadcast_to(jnp.max(s, axis=1, keepdims=True), (tile_rows, dim))
            if not first:
                old = m_ref[here]
                new = jnp.maximum(old, new)
            m_ref[here] = new
            w = jnp.exp2((s - jnp.tile(new, (1, rows // dim))) * scale)
            part = jnp.dot(w.astype(jnp.bfloat16), v_block, preferred_element_type=jnp.float32)
            if first:
                acc_ref[here] = part
            else:
                acc_ref[here] = (
                    acc_ref[here] * jnp.tile(jnp.exp2((old - new) * scale), (1, 2)) + part
                )

    def process(block):
        @pl.when((block <= me) & (block >= me - window))
        def _():
            attend(block)

    attend(me, True)
    own_pair(z)
    process(me + 1 - 2 * c)

    @pl.when(jnp.logical_not(top))
    def _():
        def ahead(i, carry):
            from_below(z - i)
            return carry

        lax.fori_loop(1, last + 1, ahead, 0)

    def step(i, carry):
        level = z - i

        @pl.when(top)
        def _():
            from_below(level)

        process(level * 4 + r)
        from_across(level + 1)
        process((level + 1) * 4 + 2 * (1 - y) + c)
        own_pair(level)
        process(level * 4 + 2 * y + 1 - c)
        other_pair(level + 1)
        process((level + 1) * 4 + 2 * (1 - y) + 1 - c)
        return carry

    lax.fori_loop(1, last + 1, step, 0)
    from_across(z - last)
    process((z - last) * 4 + 2 * (1 - y) + c)
    other_pair(z - last)
    process((z - last) * 4 + 2 * (1 - y) + 1 - c)

    for head in range(heads):
        here = slice(head * rows, (head + 1) * rows)
        o_ref[:, head * dim : (head + 1) * dim] = (acc_ref[here, :dim] / acc_ref[here, dim:]).astype(
            o_ref.dtype
        )

    def drain(i, carry):
        finish(z - i)
        return carry

    lax.fori_loop(0, last + 1, drain, 0)


def solution(mesh):
    n = mesh.shape["ctx"]

    def on_device(queries, keys, values, doc_ids):
        rows, width = queries.shape
        dim = keys.shape[1]
        heads = width // dim
        levels = n // 4
        anywhere = pl.BlockSpec(memory_space=pl.ANY)
        return pl.pallas_call(
            functools.partial(kernel, n),
            out_shape=jax.ShapeDtypeStruct((rows, width), jnp.bfloat16),
            in_specs=[anywhere] * 4,
            out_specs=pl.BlockSpec(memory_space=pltpu.VMEM),
            scratch_shapes=[
                pltpu.VMEM((rows, width), jnp.bfloat16),
                pltpu.VMEM((2, n * rows, dim), jnp.bfloat16),
                pltpu.VMEM((n, 1, rows), jnp.int32),
                pltpu.VMEM((heads * rows, dim), jnp.float32),
                pltpu.VMEM((heads * rows, 2 * dim), jnp.float32),
                pltpu.VMEM((heads * rows, 2 * dim), jnp.bfloat16),
                pltpu.SemaphoreType.DMA((4,)),
                pltpu.SemaphoreType.DMA((5, levels, 2)),
                pltpu.SemaphoreType.DMA((4, levels, 2)),
                pltpu.SemaphoreType.DMA((5, levels)),
                pltpu.SemaphoreType.DMA((4, levels)),
            ],
            compiler_params=pltpu.CompilerParams(collective_id=0, has_side_effects=True, vmem_limit_bytes=16 * 1024 * 1024),
        )(*[pltpu.with_memory_space_constraint(a, pltpu.HBM) for a in (queries, keys, values, doc_ids.reshape(1, rows))])

    spec = P(("groups", "ctx"), None)
    return jax.shard_map(
        on_device,
        mesh=mesh,
        in_specs=(spec, spec, spec, P(("groups", "ctx"))),
        out_specs=spec,
        check_vma=False,
    )
```

time: 22.5 us -> 23.5 us (1.044)
  Pallas kernels: 21.3 us -> 22.5 us
    pallas_call x1, Pallas kernels: 21.3 us -> 22.5 us  [on_device(): pl.pallas_call(functools.partial(kernel, n), out_shape=jax.ShapeDtypeStru...]
where the time goes in v1:
time: 23.5 us; the launch traced here: 23.3 us
  Pallas kernels  22.5 us (96%)
  local copies, waits for them, and re-layouts  0.8 us (3%)
    pallas_call x1, Pallas kernels, on_device(): pl.pallas_call(functools.partial(kernel, n), out_shape=jax.ShapeDtypeStru...  22.5 us
    unnamed x1, local copies, waits for them, and re-layouts  0.8 us

profile of v1, /device:TPU:25, one launch (start us, length us, event | category | flops | bytes accessed | tf_op | source)
XLA Modules:
  0.0 23.3 jit_solution(16959415844653329365)
XLA Ops:
  0.0 22.5 %shard_map.46 = bf16[256,1024]{1,0:T(8,128)(2,1)S(1)} custom-call(bf16[256,1024]{1,0:T(8,128)(2,1)} %q_hbm.1, bf16[256,128]{1,0:T(8,128)(2,1)} %k_hbm.1, bf16[256,128]{1,0:T(8,128)(2,1)} %v_hbm.1, s32[1,256]{1,0:T(1,128)} %bitcast.1), custom_call_target="tpu_custom_call" | custom-call | tf_op jit(solution)/shard_map/pallas_call | solution.py:332
  22.5 0.8 %copy.6 = bf16[256,1024]{1,0:T(8,128)(2,1)} copy(bf16[256,1024]{1,0:T(8,128)(2,1)S(1)} %shard_map.46) | data formatting | bytes 1048576

commit v2 on v1

--- a/solution.py
+++ b/solution.py
@@ -31,6 +31,7 @@
     recv_kv,
     send_doc,
     recv_doc,
+    ready_sem,
 ):
     rows, width = q_hbm.shape
     dim = k_hbm.shape[1]
@@ -50,6 +51,10 @@
     scale = dim ** (-0.5) * LOG2E
     top = z == levels - 1
     last = jnp.minimum(z, depth)
+    quick = levels == 4
+    source = (z == 1) & (y == 1) if quick else False
+    aside = (z == 2) & (y == 0) if quick else False
+    beyond = (z == 3) & (y == 1) if quick else False
 
     barrier = pltpu.get_barrier_semaphore()
 
@@ -68,6 +73,15 @@
 
     greet(across)
     greet(partner)
+    if quick:
+
+        @pl.when(aside)
+        def _():
+            greet(me - 2)
+
+        @pl.when(source)
+        def _():
+            greet(me + 8)
 
     def span(block):
         return pl.ds(pl.multiple_of(block * rows, rows), rows)
@@ -124,11 +138,15 @@
     def from_under(some_z, some_y, level):
         return (some_y == 0) & (some_z - level == depth) & needs(2 * some_z, 2 * level + 1)
 
+    def spared(level):
+        return (z == 2) & (y == 1) & (level == 0) if quick else False
+
     def climbs(level):
-        return (z < levels - 1) & (z - level < depth)
+        return (z < levels - 1) & (z - level < depth) & jnp.logical_not(spared(level))
 
     def crosses(level):
-        return needs(2 * z + 1 - y, 2 * level + y) & jnp.logical_not(from_under(z, 1 - y, level))
+        direct = needs(2 * z + 1 - y, 2 * level + y) & jnp.logical_not(from_under(z, 1 - y, level))
+        return direct & jnp.logical_not(spared(level))
 
     def crossed(level):
         return needs(chip, 2 * level + 1 - y)
@@ -154,9 +172,28 @@
         start(2, 2, level, piece, own(level), partner)
 
     def from_below(level):
-        for piece in range(2):
-            arrived(0, level, piece, own(level), up)
-            relay(level, piece)
+        def plain():
+            for piece in range(2):
+                arrived(0, level, piece, own(level), up)
+                relay(level, piece)
+
+        if not quick:
+            plain()
+            return
+        pl.when(jnp.logical_not(source))(plain)
+
+        @pl.when(source)
+        def _():
+            for piece in range(2):
+                arrived(0, level, piece, own(level), up)
+                start(4, 1, level, piece, own(level), me + 2)
+                start(1, 1, level, piece, own(level), across)
+                start(2, 2, level, piece, own(level), partner)
+            for piece in range(2):
+                start(0, 0, level, piece, own(level), up)
+            pl.semaphore_wait(ready_sem, 1)
+            for piece in range(2):
+                start(5, 0, level, piece, own(level), me + 8)
 
     def from_across(level):
         @pl.when(crossed(level))
@@ -192,6 +229,12 @@
                 sent(1, 1, level, piece, own(level), across)
 
             sent(2, 2, level, piece, own(level), partner)
+            if quick:
+
+                @pl.when(source & (level == 0))
+                def _():
+                    sent(4, 1, level, piece, own(level), me + 2)
+                    sent(5, 0, level, piece, own(level), me + 8)
 
             @pl.when(crossed(level))
             def _():
@@ -201,7 +244,18 @@
                 def _():
                     sent(4, 1, level, piece, other(level), up)
 
-    pl.semaphore_wait(barrier, 2 + jnp.minimum(z, 1) + jnp.minimum(levels - 1 - z, 1))
+    greeters = 2 + jnp.minimum(z, 1) + jnp.minimum(levels - 1 - z, 1)
+    if quick:
+        greeters = greeters + jnp.where(source | beyond, 1, 0)
+    pl.semaphore_wait(barrier, greeters)
+    if quick:
+
+        @pl.when(beyond)
+        def _():
+            pl.semaphore_signal(
+                ready_sem, inc=1, device_id={"ctx": me - 8}, device_id_type=pl.DeviceIdType.MESH
+            )
+
     for fill in fills[:1] + fills[2:]:
         fill.wait()
     relay(z, 0)
@@ -229,11 +283,16 @@
     tile_rows = TILE_HEADS * rows
     tiles = heads // TILE_HEADS
 
-    def attend(block, first=False):
-        place = span(block)
-        marks = jnp.where(lane == doc_of(block), 1.0, 0.0).astype(jnp.bfloat16)
-        k_block = jnp.concatenate([kv[0, place, :], marks], axis=1)
-        v_block = jnp.concatenate([kv[1, place, :], jnp.ones((rows, dim), jnp.bfloat16)], axis=1)
+    def attend(blocks, first=False):
+        ks, vs = [], []
+        for block in blocks:
+            place = span(block)
+            marks = jnp.where(lane == doc_of(block), 1.0, 0.0).astype(jnp.bfloat16)
+            ks.append(jnp.concatenate([kv[0, place, :], marks], axis=1))
+            vs.append(jnp.concatenate([kv[1, place, :], jnp.ones((rows, dim), jnp.bfloat16)], axis=1))
+        k_block = jnp.concatenate(ks, axis=0)
+        v_block = jnp.concatenate(vs, axis=0)
+        length = k_block.shape[0]
 
         def scores(tile):
             return lax.dot_general(
@@ -259,7 +318,7 @@
                 old = m_ref[here]
                 new = jnp.maximum(old, new)
             m_ref[here] = new
-            w = jnp.exp2((s - jnp.tile(new, (1, rows // dim))) * scale)
+            w = jnp.exp2((s - jnp.tile(new, (1, length // dim))) * scale)
             part = jnp.dot(w.astype(jnp.bfloat16), v_block, preferred_element_type=jnp.float32)
             if first:
                 acc_ref[here] = part
@@ -268,44 +327,61 @@
                     acc_ref[here] * jnp.tile(jnp.exp2((old - new) * scale), (1, 2)) + part
                 )
 
-    def process(block):
-        @pl.when((block <= me) & (block >= me - window))
-        def _():
-            attend(block)
-
-    attend(me, True)
+    def process(chunk):
+        @pl.when((chunk <= chip) & (2 * chunk + 1 >= me - window))
+        def _():
+            attend([2 * chunk, 2 * chunk + 1])
+
+    attend([me], True)
     own_pair(z)
-    process(me + 1 - 2 * c)
-
-    @pl.when(jnp.logical_not(top))
+
+    @pl.when(c == 1)
     def _():
-        def ahead(i, carry):
-            from_below(z - i)
-            return carry
-
-        lax.fori_loop(1, last + 1, ahead, 0)
-
-    def step(i, carry):
-        level = z - i
-
-        @pl.when(top)
-        def _():
-            from_below(level)
-
-        process(level * 4 + r)
-        from_across(level + 1)
-        process((level + 1) * 4 + 2 * (1 - y) + c)
-        own_pair(level)
-        process(level * 4 + 2 * y + 1 - c)
-        other_pair(level + 1)
-        process((level + 1) * 4 + 2 * (1 - y) + 1 - c)
+        attend([me - 1])
+
+    def early(level):
+        return jnp.logical_not(top) & (climbs(level) | crosses(level))
+
+    def ahead(i, carry):
+        pl.when(early(z - i))(lambda: from_below(z - i))
         return carry
 
-    lax.fori_loop(1, last + 1, step, 0)
-    from_across(z - last)
-    process((z - last) * 4 + 2 * (1 - y) + c)
+    lax.fori_loop(1, last + 1, ahead, 0)
+
+    for i in range(1, depth + 1):
+
+        @pl.when(z >= i)
+        def _():
+            level = z - i
+            final = (z == i) | (i == depth)
+            late = final & (y == 1)
+            before = jnp.logical_not(late)
+            hooked = top & before if i > 1 else False
+            waits = jnp.logical_not(early(level) | hooked)
+
+            def own_set():
+                pl.when(waits)(lambda: from_below(level))
+                own_pair(level)
+
+            from_across(level + 1)
+            pl.when(final & jnp.logical_not(top))(lambda: from_across(level))
+            pl.when(before)(own_set)
+            pl.when(late)(lambda: other_pair(level + 1))
+            ours, theirs = 2 * level + y, 2 * (level + 1) + 1 - y
+            process(jnp.where(late, theirs, ours))
+            if i < depth:
+                soon = (z == i + 1) | (i + 1 == depth)
+                pl.when(top & jnp.logical_not(final) & jnp.logical_not(soon & (y == 1)))(
+                    lambda: from_below(level - 1)
+                )
+            pl.when(final & top)(lambda: from_across(level))
+            pl.when(late)(own_set)
+            pl.when(before)(lambda: other_pair(level + 1))
+            process(jnp.where(late, ours, theirs))
+
+    pl.when(z == 0)(lambda: from_across(z))
     other_pair(z - last)
-    process((z - last) * 4 + 2 * (1 - y) + 1 - c)
+    process(2 * (z - last) + 1 - y)
 
     for head in range(heads):
         here = slice(head * rows, (head + 1) * rows)
@@ -342,10 +418,11 @@
                 pltpu.VMEM((heads * rows, 2 * dim), jnp.float32),
                 pltpu.VMEM((heads * rows, 2 * dim), jnp.bfloat16),
                 pltpu.SemaphoreType.DMA((4,)),
-                pltpu.SemaphoreType.DMA((5, levels, 2)),
+                pltpu.SemaphoreType.DMA((6, levels, 2)),
                 pltpu.SemaphoreType.DMA((4, levels, 2)),
-                pltpu.SemaphoreType.DMA((5, levels)),
+                pltpu.SemaphoreType.DMA((6, levels)),
                 pltpu.SemaphoreType.DMA((4, levels)),
+                pltpu.SemaphoreType.REGULAR,
             ],
             compiler_params=pltpu.CompilerParams(collective_id=0, has_side_effects=True, vmem_limit_bytes=16 * 1024 * 1024),
         )(*[pltpu.with_memory_space_constraint(a, pltpu.HBM) for a in (queries, keys, values, doc_ids.reshape(1, rows))])

time: 23.5 us -> 21.9 us (0.932)
  Pallas kernels: 22.5 us -> 20.7 us
    pallas_call x1, Pallas kernels: 22.5 us -> 20.7 us  [on_device(): pl.pallas_call(functools.partial(kernel, n), out_shape=jax.ShapeDtypeStru...]
where the time goes in v2:
time: 21.9 us; the launch traced here: 21.5 us
  Pallas kernels  20.7 us (95%)
  local copies, waits for them, and re-layouts  0.8 us (4%)
    pallas_call x1, Pallas kernels, on_device(): pl.pallas_call(functools.partial(kernel, n), out_shape=jax.ShapeDtypeStru...  20.7 us
    unnamed x1, local copies, waits for them, and re-layouts  0.8 us

profile of v2, /device:TPU:25, one launch (start us, length us, event | category | flops | bytes accessed | tf_op | source)
XLA Modules:
  0.0 21.5 jit_solution(8625025678678266657)
XLA Ops:
  0.0 20.7 %shard_map.46 = bf16[256,1024]{1,0:T(8,128)(2,1)S(1)} custom-call(bf16[256,1024]{1,0:T(8,128)(2,1)} %q_hbm.1, bf16[256,128]{1,0:T(8,128)(2,1)} %k_hbm.1, bf16[256,128]{1,0:T(8,128)(2,1)} %v_hbm.1, s32[1,256]{1,0:T(1,128)} %bitcast.1), custom_call_target="tpu_custom_call" | custom-call | tf_op jit(solution)/shard_map/pallas_call | solution.py:408
  20.7 0.8 %copy.6 = bf16[256,1024]{1,0:T(8,128)(2,1)} copy(bf16[256,1024]{1,0:T(8,128)(2,1)S(1)} %shard_map.46) | data formatting | bytes 1048576

commit v3 on v2

v3 whole, which is shorter than its diff:
```python
import functools

import jax
import jax.numpy as jnp
from jax import lax
from jax.experimental import pallas as pl
from jax.experimental.pallas import tpu as pltpu
from jax.sharding import PartitionSpec as P

HIDDEN = -1e30
LOG2E = 1.4426950408889634
DOCS = 3
DOC_ROWS = 16
PIECES = 4
TILE_HEADS = 2


def kernel(
    n,
    q_hbm,
    k_hbm,
    v_hbm,
    d_hbm,
    o_ref,
    q_ref,
    kv,
    docs,
    m_ref,
    acc_ref,
    qs,
    fill_sem,
    send_kv,
    recv_kv,
    recv_pair,
    send_far,
    ready_sem,
):
    rows, width = q_hbm.shape
    dim = k_hbm.shape[1]
    heads = width // dim
    levels = n // 4
    window = 3 * n // 4
    depth = (window + 3) // 4
    me = lax.axis_index("ctx")
    z = me // 4
    r = me % 4
    y = r // 2
    c = r % 2
    chip = me // 2
    up = me + 4
    across = z * 4 + (1 - y) * 2 + c
    partner = z * 4 + y * 2 + (1 - c)
    scale = dim ** (-0.5) * LOG2E
    top = z == levels - 1
    tail = top & (z >= depth)
    last = jnp.minimum(z, depth)
    quick = levels == 4
    source = (z == 1) & (y == 1) if quick else False
    aside = (z == 2) & (y == 0) if quick else False
    beyond = (z == 3) & (y == 1) if quick else False

    barrier = pltpu.get_barrier_semaphore()

    def greet(device):
        pl.semaphore_signal(
            barrier, inc=1, device_id={"ctx": device}, device_id_type=pl.DeviceIdType.MESH
        )

    @pl.when(z > 0)
    def _():
        greet(me - 4)

    @pl.when(z < levels - 1)
    def _():
        greet(up)

    greet(across)
    greet(partner)
    if quick:

        @pl.when(aside)
        def _():
            greet(me - 2)

        @pl.when(source)
        def _():
            greet(me + 8)

    assert rows <= 256 and rows % dim == 0
    stride = 2 * rows + DOC_ROWS
    half = rows // 2
    pieces = [(0, half), (half, half + DOC_ROWS), (rows + DOC_ROWS, half), (rows + DOC_ROWS + half, half)]

    def span(block, first=0, count=stride):
        return pl.ds(pl.multiple_of(block * stride + first, DOC_ROWS), count)

    doc_fill = pltpu.make_async_copy(d_hbm, docs, fill_sem.at[2])
    doc_fill.start()
    fills = [
        pltpu.make_async_copy(k_hbm, kv.at[span(me, 0, rows), :], fill_sem.at[0]),
        pltpu.make_async_copy(v_hbm, kv.at[span(me, rows + DOC_ROWS, rows), :], fill_sem.at[1]),
    ]
    for fill in fills:
        fill.start()
    query_fill = pltpu.make_async_copy(q_hbm, q_ref, fill_sem.at[3])
    query_fill.start()

    def landing(lands, level, piece):
        return recv_kv.at[lands, level, piece] if lands < 2 else recv_pair.at[lands - 2, level]

    def copy_of(stream, lands, level, piece, block, device):
        place = span(block) if piece is None else span(block, *pieces[piece])
        return pltpu.make_async_remote_copy(
            src_ref=kv.at[place, :],
            dst_ref=kv.at[place, :],
            send_sem=send_kv.at[stream, level] if stream < 4 else send_far.at[stream - 4],
            recv_sem=landing(lands, level, piece),
            device_id={"ctx": device},
            device_id_type=pl.DeviceIdType.MESH,
        )

    def start(stream, lands, level, piece, block, device):
        copy_of(stream, lands, level, piece, block, device).start()

    def arrived(lands, level, piece, block, device):
        copy_of(lands, lands, level, piece, block, device).wait_recv()

    def sent(stream, level, block, device):
        copy_of(stream, 2, level, None, block, device).wait_send()

    def needs(some_chip, chunk):
        return (chunk <= some_chip) & (2 * chunk + 1 >= 2 * some_chip - window)

    def from_under(some_z, some_y, level):
        return (some_y == 0) & (some_z - level == depth) & needs(2 * some_z, 2 * level + 1)

    def spared(level):
        return (z == 2) & (y == 1) & (level == 0) if quick else False

    def climbs(level):
        return (z < levels - 1) & (z - level < depth) & jnp.logical_not(spared(level))

    def crosses(level):
        direct = needs(2 * z + 1 - y, 2 * level + y) & jnp.logical_not(from_under(z, 1 - y, level))
        return direct & jnp.logical_not(spared(level))

    def crossed(level):
        return needs(chip, 2 * level + 1 - y)

    def passes(level):
        return (z < levels - 1) & from_under(z + 1, y, level)

    def own(level):
        return level * 4 + r

    def other(level):
        return level * 4 + 2 * (1 - y) + c

    def relay(level, piece):
        @pl.when(climbs(level))
        def _():
            start(0, 0, level, piece, own(level), up)

        @pl.when(crosses(level))
        def _():
            start(1, 1, level, piece, own(level), across)

        start(2, 2, level, piece, own(level), partner)

    def from_below(level):
        def plain():
            for piece in range(len(pieces)):
                arrived(0, level, piece, own(level), up)
                relay(level, piece)

        if not quick:
            plain()
            return
        pl.when(jnp.logical_not(source))(plain)

        @pl.when(source)
        def _():
            for piece in range(len(pieces)):
                arrived(0, level, piece, own(level), up)
                start(4, 1, level, piece, own(level), me + 2)
                start(1, 1, level, piece, own(level), across)
                start(2, 2, level, piece, own(level), partner)
            for piece in range(len(pieces)):
                start(0, 0, level, piece, own(level), up)
            pl.semaphore_wait(ready_sem, 1)
            for piece in range(len(pieces)):
                start(5, 0, level, piece, own(level), me + 8)

    def from_across(level):
        @pl.when(crossed(level))
        def _():
            for piece in range(len(pieces)):
                arrived(1, level, piece, other(level), across)

                @pl.when(passes(level))
                def _():
                    start(4, 1, level, piece, other(level), up)

                start(3, 3, level, piece, other(level), partner)

    def own_pair(level):
        arrived(2, level, None, level * 4 + 2 * y + 1 - c, partner)

    def other_pair(level):
        @pl.when(crossed(level))
        def _():
            arrived(3, level, None, level * 4 + 2 * (1 - y) + 1 - c, partner)

    def finish(level):
        @pl.when(climbs(level))
        def _():
            sent(0, level, own(level), up)

        @pl.when(crosses(level))
        def _():
            sent(1, level, own(level), across)

        sent(2, level, own(level), partner)
        if quick:

            @pl.when(source & (level == 0))
            def _():
                sent(4, level, own(level), me + 2)
                sent(5, level, own(level), me + 8)

        @pl.when(crossed(level))
        def _():
            sent(3, level, other(level), partner)

            @pl.when(passes(level))
            def _():
                sent(4, level, other(level), up)

    doc_fill.wait()
    ids = docs[...]
    bounds = [jnp.sum(jnp.where(ids < doc, 1.0, 0.0), keepdims=True) for doc in range(1, DOCS)]
    bounds = [jnp.broadcast_to(bound, (1, dim)) for bound in bounds]
    bounds.append(jnp.zeros((DOC_ROWS - len(bounds), dim), jnp.float32))
    kv[span(me, rows, DOC_ROWS), :] = jnp.concatenate(bounds, axis=0).astype(jnp.bfloat16)
    greeters = 2 + jnp.minimum(z, 1) + jnp.minimum(levels - 1 - z, 1)
    if quick:
        greeters = greeters + jnp.where(source | beyond, 1, 0)
    pl.semaphore_wait(barrier, greeters)
    if quick:

        @pl.when(beyond)
        def _():
            pl.semaphore_signal(
                ready_sem, inc=1, device_id={"ctx": me - 8}, device_id_type=pl.DeviceIdType.MESH
            )

    fills[0].wait()
    for piece in range(len(pieces)):
        if pieces[piece][0] == rows + DOC_ROWS:
            fills[1].wait()
        relay(z, piece)

    lane = lax.broadcasted_iota(jnp.int32, (rows, dim), 1)
    row = lax.broadcasted_iota(jnp.int32, (rows, dim), 0).astype(jnp.float32)

    def doc_of(block):
        bounds = kv[span(block, rows, DOC_ROWS), :].astype(jnp.float32)
        number = jnp.zeros((rows, dim), jnp.int32)
        for doc in range(1, DOCS):
            number = number + jnp.where(row >= bounds[doc - 1 : doc, :], 1, 0)
        return number

    query_marks = jnp.where(lane == doc_of(me), 0.0, HIDDEN).astype(jnp.bfloat16)
    query_fill.wait()
    for head in range(heads):
        here = slice(head * rows, (head + 1) * rows)
        qs[here, :dim] = q_ref[:, head * dim : (head + 1) * dim]
        qs[here, dim:] = query_marks

    tile_rows = TILE_HEADS * rows
    tiles = heads // TILE_HEADS

    def attend(blocks, first=False):
        ks, vs = [], []
        for block in blocks:
            marks = jnp.where(lane == doc_of(block), 1.0, 0.0).astype(jnp.bfloat16)
            ks.append(jnp.concatenate([kv[span(block, 0, rows), :], marks], axis=1))
            vs.append(jnp.concatenate([kv[span(block, rows + DOC_ROWS, rows), :], jnp.ones((rows, dim), jnp.bfloat16)], axis=1))
        k_block = jnp.concatenate(ks, axis=0)
        v_block = jnp.concatenate(vs, axis=0)
        length = k_block.shape[0]

        def scores(tile):
            return lax.dot_general(
                qs[tile * tile_rows : (tile + 1) * tile_rows, :],
                k_block,
                (((1,), (1,)), ((), ())),
                preferred_element_type=jnp.float32,
            )

        following = scores(0)
        for tile in range(tiles):
            s = following
            if tile + 1 < tiles:
                following = scores(tile + 1)
            here = slice(tile * tile_rows, (tile + 1) * tile_rows)
            if first:
                key_id = lax.broadcasted_iota(jnp.int32, (rows, rows), 1)
                query_id = lax.broadcasted_iota(jnp.int32, (rows, rows), 0)
                hide = jnp.where(key_id <= query_id, 0.0, HIDDEN)
                s = s + jnp.concatenate([hide] * TILE_HEADS, axis=0)
            new = jnp.broadcast_to(jnp.max(s, axis=1, keepdims=True), (tile_rows, dim))
            if not first:
                old = m_ref[here]
                new = jnp.maximum(old, new)
            m_ref[here] = new
            w = jnp.exp2((s - jnp.tile(new, (1, length // dim))) * scale)
            part = jnp.dot(w.astype(jnp.bfloat16), v_block, preferred_element_type=jnp.float32)
            if first:
                acc_ref[here] = part
            else:
                acc_ref[here] = (
                    acc_ref[here] * jnp.tile(jnp.exp2((old - new) * scale), (1, 2)) + part
                )

    attend([me], True)
    own_pair(z)

    @pl.when(c == 1)
    def _():
        attend([me - 1])

    def early(level):
        return jnp.logical_not(top) & (climbs(level) | crosses(level))

    def ahead(i, carry):
        pl.when(early(z - i))(lambda: from_below(z - i))
        return carry

    lax.fori_loop(1, last + 1, ahead, 0)

    def pair_of(level):
        return level * 4 + 2 * y + 1 - c

    def other_pair_of(level):
        return level * 4 + 2 * (1 - y) + 1 - c

    for i in range(1, depth + 1):

        @pl.when(z >= i)
        def _():
            level = z - i
            final = (z == i) | (i == depth)
            late = final & (y == 1)
            single = late & tail
            pairs = late & jnp.logical_not(tail)
            before = jnp.logical_not(late)
            both = before & crossed(level + 1)
            hooked = top & (y == 1) if i > 1 else False
            waits = jnp.logical_not(early(level))

            pl.when(before & waits & jnp.logical_not(hooked))(lambda: from_below(level))
            from_across(level + 1)
            pl.when(final & jnp.logical_not(top))(lambda: from_across(level))
            pl.when(pairs)(lambda: other_pair(level + 1))

            @pl.when(both | pairs)
            def _():
                attend(
                    [
                        jnp.where(both, own(level), other(level + 1)),
                        jnp.where(both, other(level + 1), other_pair_of(level + 1)),
                    ]
                )

            pl.when(pairs & waits)(lambda: from_below(level))
            if i + 1 < depth:
                last_but = z == i + 1
                pl.when(top & (y == 1) & jnp.logical_not(final | last_but))(
                    lambda: from_below(level - 1)
                )

            @pl.when(jnp.logical_not(single))
            def _():
                own_pair(level)
                pl.when(both)(lambda: other_pair(level + 1))
                attend(
                    [
                        jnp.where(both, pair_of(level), own(level)),
                        jnp.where(both, other_pair_of(level + 1), pair_of(level)),
                    ]
                )

    pl.when(z == 0)(lambda: from_across(z))

    @pl.when(jnp.logical_not(tail))
    def _():
        @pl.when(crossed(z - last))
        def _():
            other_pair(z - last)
            attend([other(z - last), other_pair_of(z - last)])

    def closing(turn, carry):
        level = z - last

        @pl.when(turn == 1)
        def _():
            from_below(level)
            other_pair(level + 1)

        pl.when(turn == 3)(lambda: own_pair(level))
        pl.when(turn == 4)(lambda: from_across(level))
        pl.when(turn == 5)(lambda: other_pair(level))
        theirs = (turn < 2) | (turn > 3)
        base = (level + jnp.where(turn < 2, 1, 0)) * 4 + 2 * jnp.where(theirs, 1 - y, y)
        block = base + jnp.where(turn % 2 == 0, c, 1 - c)

        @pl.when((block <= me) & (block >= me - window))
        def _():
            attend([block])

        return carry

    @pl.when(tail)
    def _():
        lax.fori_loop(4 - 4 * y, 6 - 2 * y, closing, 0)

    for head in range(heads):
        here = slice(head * rows, (head + 1) * rows)
        o_ref[:, head * dim : (head + 1) * dim] = (acc_ref[here, :dim] / acc_ref[here, dim:]).astype(
            o_ref.dtype
        )

    def drain(i, carry):
        finish(z - i)
        return carry

    lax.fori_loop(0, last + 1, drain, 0)


def solution(mesh):
    n = mesh.shape["ctx"]

    def on_device(queries, keys, values, doc_ids):
        rows, width = queries.shape
        dim = keys.shape[1]
        heads = width // dim
        levels = n // 4
        anywhere = pl.BlockSpec(memory_space=pl.ANY)
        return pl.pallas_call(
            functools.partial(kernel, n),
            out_shape=jax.ShapeDtypeStruct((rows, width), jnp.bfloat16),
            in_specs=[anywhere] * 4,
            out_specs=pl.BlockSpec(memory_space=pltpu.VMEM),
            scratch_shapes=[
                pltpu.VMEM((rows, width), jnp.bfloat16),
                pltpu.VMEM((n * (2 * rows + DOC_ROWS), dim), jnp.bfloat16),
                pltpu.VMEM((rows // dim, dim), jnp.int32),
                pltpu.VMEM((heads * rows, dim), jnp.float32),
                pltpu.VMEM((heads * rows, 2 * dim), jnp.float32),
                pltpu.VMEM((heads * rows, 2 * dim), jnp.bfloat16),
                pltpu.SemaphoreType.DMA((4,)),
                pltpu.SemaphoreType.DMA((4, levels)),
                pltpu.SemaphoreType.DMA((2, levels, PIECES)),
                pltpu.SemaphoreType.DMA((2, levels)),
                pltpu.SemaphoreType.DMA((2,)),
                pltpu.SemaphoreType.REGULAR,
            ],
            compiler_params=pltpu.CompilerParams(collective_id=0, has_side_effects=True, vmem_limit_bytes=16 * 1024 * 1024),
        )(*[pltpu.with_memory_space_constraint(a, pltpu.HBM) for a in (queries, keys, values, doc_ids.reshape(rows // dim, dim))])

    spec = P(("groups", "ctx"), None)
    return jax.shard_map(
        on_device,
        mesh=mesh,
        in_specs=(spec, spec, spec, P(("groups", "ctx"))),
        out_specs=spec,
        check_vma=False,
    )
```

time: 21.9 us -> 20.6 us (0.941); the launches traced: 21.5 us -> 20.4 us
  Pallas kernels: 20.7 us -> 19.6 us
    pallas_call x1, Pallas kernels: 20.7 us -> 19.6 us  [on_device(): pl.pallas_call(functools.partial(kernel, n), out_shape=jax.ShapeDtypeStru...]
where the time goes in v3:
time: 20.6 us; the launch traced here: 20.4 us
  Pallas kernels  19.6 us (95%)
  local copies, waits for them, and re-layouts  0.8 us (4%)
    pallas_call x1, Pallas kernels, on_device(): pl.pallas_call(functools.partial(kernel, n), out_shape=jax.ShapeDtypeStru...  19.6 us
    unnamed x1, local copies, waits for them, and re-layouts  0.8 us

profile of v3, /device:TPU:25, one launch (start us, length us, event | category | flops | bytes accessed | tf_op | source)
XLA Modules:
  0.0 20.4 jit_solution(14899048748011342361)
XLA Ops:
  0.0 19.6 %shard_map.46 = bf16[256,1024]{1,0:T(8,128)(2,1)S(1)} custom-call(bf16[256,1024]{1,0:T(8,128)(2,1)} %q_hbm.1, bf16[256,128]{1,0:T(8,128)(2,1)} %k_hbm.1, bf16[256,128]{1,0:T(8,128)(2,1)} %v_hbm.1, s32[2,128]{1,0:T(2,128)} %bitcast.1), custom_call_target="tpu_custom_call" | custom-call | tf_op jit(solution)/shard_map/pallas_call | solution.py:450
  19.7 0.8 %copy.6 = bf16[256,1024]{1,0:T(8,128)(2,1)} copy(bf16[256,1024]{1,0:T(8,128)(2,1)S(1)} %shard_map.46) | data formatting | bytes 1048576

commit v4 on v3

--- a/solution.py
+++ b/solution.py
@@ -165,7 +165,8 @@
         def _():
             start(1, 1, level, piece, own(level), across)
 
-        start(2, 2, level, piece, own(level), partner)
+        if piece == len(pieces) - 1:
+            start(2, 2, level, None, own(level), partner)
 
     def from_below(level):
         def plain():
@@ -184,7 +185,7 @@
                 arrived(0, level, piece, own(level), up)
                 start(4, 1, level, piece, own(level), me + 2)
                 start(1, 1, level, piece, own(level), across)
-                start(2, 2, level, piece, own(level), partner)
+            start(2, 2, level, None, own(level), partner)
             for piece in range(len(pieces)):
                 start(0, 0, level, piece, own(level), up)
             pl.semaphore_wait(ready_sem, 1)
@@ -201,7 +202,7 @@
                 def _():
                     start(4, 1, level, piece, other(level), up)
 
-                start(3, 3, level, piece, other(level), partner)
+            start(3, 3, level, None, other(level), partner)
 
     def own_pair(level):
         arrived(2, level, None, level * 4 + 2 * y + 1 - c, partner)
@@ -352,16 +353,19 @@
             level = z - i
             final = (z == i) | (i == depth)
             late = final & (y == 1)
-            single = late & tail
             pairs = late & jnp.logical_not(tail)
-            before = jnp.logical_not(late)
+            before = jnp.logical_not(pairs)
             both = before & crossed(level + 1)
             hooked = top & (y == 1) if i > 1 else False
             waits = jnp.logical_not(early(level))
 
-            pl.when(before & waits & jnp.logical_not(hooked))(lambda: from_below(level))
+            closing = late & tail
+            pl.when(before & waits & jnp.logical_not(hooked | closing))(lambda: from_below(level))
+            far = final & jnp.logical_not(top) & (y == 0)
+            pl.when(far)(lambda: from_across(level))
             from_across(level + 1)
-            pl.when(final & jnp.logical_not(top))(lambda: from_across(level))
+            pl.when(closing)(lambda: from_below(level))
+            pl.when(pairs)(lambda: from_across(level))
             pl.when(pairs)(lambda: other_pair(level + 1))
 
             @pl.when(both | pairs)
@@ -373,57 +377,46 @@
                     ]
                 )
 
-            pl.when(pairs & waits)(lambda: from_below(level))
             if i + 1 < depth:
                 last_but = z == i + 1
                 pl.when(top & (y == 1) & jnp.logical_not(final | last_but))(
                     lambda: from_below(level - 1)
                 )
 
-            @pl.when(jnp.logical_not(single))
+            pl.when(final & tail)(lambda: from_across(level))
+            pl.when(pairs & waits)(lambda: from_below(level))
+
+            @pl.when(before | crossed(level))
             def _():
-                own_pair(level)
+                pl.when(before)(lambda: own_pair(level))
                 pl.when(both)(lambda: other_pair(level + 1))
+                pl.when(pairs)(lambda: other_pair(level))
                 attend(
                     [
-                        jnp.where(both, pair_of(level), own(level)),
-                        jnp.where(both, other_pair_of(level + 1), pair_of(level)),
+                        jnp.where(both, pair_of(level), jnp.where(pairs, other(level), own(level))),
+                        jnp.where(
+                            both,
+                            other_pair_of(level + 1),
+                            jnp.where(pairs, other_pair_of(level), pair_of(level)),
+                        ),
                     ]
                 )
 
-    pl.when(z == 0)(lambda: from_across(z))
-
-    @pl.when(jnp.logical_not(tail))
+    level = z - last
+    pairs = (y == 1) & (z > 0) & jnp.logical_not(tail)
+    pl.when((z == 0) | (top & jnp.logical_not(tail) & (y == 0)))(lambda: from_across(level))
+
+    pl.when(pairs)(lambda: own_pair(level))
+    pl.when(jnp.logical_not(pairs))(lambda: other_pair(level))
+
+    @pl.when(pairs | crossed(level))
     def _():
-        @pl.when(crossed(z - last))
-        def _():
-            other_pair(z - last)
-            attend([other(z - last), other_pair_of(z - last)])
-
-    def closing(turn, carry):
-        level = z - last
-
-        @pl.when(turn == 1)
-        def _():
-            from_below(level)
-            other_pair(level + 1)
-
-        pl.when(turn == 3)(lambda: own_pair(level))
-        pl.when(turn == 4)(lambda: from_across(level))
-        pl.when(turn == 5)(lambda: other_pair(level))
-        theirs = (turn < 2) | (turn > 3)
-        base = (level + jnp.where(turn < 2, 1, 0)) * 4 + 2 * jnp.where(theirs, 1 - y, y)
-        block = base + jnp.where(turn % 2 == 0, c, 1 - c)
-
-        @pl.when((block <= me) & (block >= me - window))
-        def _():
-            attend([block])
-
-        return carry
-
-    @pl.when(tail)
-    def _():
-        lax.fori_loop(4 - 4 * y, 6 - 2 * y, closing, 0)
+        attend(
+            [
+                jnp.where(pairs, own(level), other(level)),
+                jnp.where(pairs, pair_of(level), other_pair_of(level)),
+            ]
+        )
 
     for head in range(heads):
         here = slice(head * rows, (head + 1) * rows)

time: 20.6 us -> 19.7 us (0.956)
  Pallas kernels: 19.6 us -> 18.8 us
    pallas_call x1, Pallas kernels: 19.6 us -> 18.8 us  [on_device(): pl.pallas_call(functools.partial(kernel, n), out_shape=jax.ShapeDtypeStru...]
where the time goes in v4:
time: 19.7 us; the launch traced here: 19.6 us
  Pallas kernels  18.8 us (95%)
  local copies, waits for them, and re-layouts  0.8 us (4%)
    pallas_call x1, Pallas kernels, on_device(): pl.pallas_call(functools.partial(kernel, n), out_shape=jax.ShapeDtypeStru...  18.8 us
    unnamed x1, local copies, waits for them, and re-layouts  0.8 us

profile of v4, /device:TPU:25, one launch (start us, length us, event | category | flops | bytes accessed | tf_op | source)
XLA Modules:
  0.0 19.6 jit_solution(18120135139341286469)
XLA Ops:
  0.0 18.8 %shard_map.46 = bf16[256,1024]{1,0:T(8,128)(2,1)S(1)} custom-call(bf16[256,1024]{1,0:T(8,128)(2,1)} %q_hbm.1, bf16[256,128]{1,0:T(8,128)(2,1)} %k_hbm.1, bf16[256,128]{1,0:T(8,128)(2,1)} %v_hbm.1, s32[2,128]{1,0:T(2,128)} %bitcast.1), custom_call_target="tpu_custom_call" | custom-call | tf_op jit(solution)/shard_map/pallas_call | solution.py:443
  18.8 0.8 %copy.6 = bf16[256,1024]{1,0:T(8,128)(2,1)} copy(bf16[256,1024]{1,0:T(8,128)(2,1)S(1)} %shard_map.46) | data formatting | bytes 1048576
